TPU v7x, 32 devices: a whole 2x2x4 slice. The times are simulated.
32 devices in a mesh: seq: 16 (over z, y, x), mdl: 2 (over core).
Axes of the slice: x: 2, y: 2, z: 4, core: 2. Of those that a mesh axis runs over, the one named last changes fastest.
Arguments:
- hidden_in: bfloat16 [32, 4, 2048], P(None, None, 'seq'), may hold values from -25 to 25
- cache_keys: bfloat16 [32, 512, 2048], P(None, 'seq', 'mdl'), may hold values from -250 to 250, as said below
- cache_values: bfloat16 [32, 512, 2048], P(None, 'seq', 'mdl'), may hold values from -6 to 6
- lengths: int32 [32], replicated, may hold values from 1 to 508, as said below
- query_weight: bfloat16 [2048, 2048], P('seq', 'mdl'), may hold values from -0.125 to 0.125
- key_weight: bfloat16 [2048, 2048], P('seq', 'mdl'), may hold values from -0.125 to 0.125
- value_weight: bfloat16 [2048, 2048], P('seq', 'mdl'), may hold values from -0.125 to 0.125
- out_weight: bfloat16 [2048, 2048], P('mdl', 'seq'), may hold values from -0.125 to 0.125
- gate_weight: bfloat16 [2048, 8192], P('seq', 'mdl'), may hold values from -0.125 to 0.125
- up_weight: bfloat16 [2048, 8192], P('seq', 'mdl'), may hold values from -0.125 to 0.125
- down_weight: bfloat16 [8192, 2048], P('mdl', 'seq'), may hold values from -0.0625 to 0.0625
Outputs:
- hidden_out: bfloat16 [32, 4, 2048], P(None, None, 'seq')
- new_cache_keys: bfloat16 [32, 512, 2048], P(None, 'seq', 'mdl')
- new_cache_values: bfloat16 [32, 512, 2048], P(None, 'seq', 'mdl')
Inputs may be any that keep to these rules, and one draw needn't show every extreme that they name: `cache_keys`: keys are stored after their rotary embedding. `lengths`: at least one request has exactly 508 cached positions.
All inputs are finite; a program needn't handle non-finite values.
Results may differ from a plain program's by a relative error of at most 0.012.
The roundings to bfloat16 on the way count: a program that leaves them out, or rounds other values in their place, can miss the bound.
Values may be sent and summed in bfloat16 or wider, within the bound.
A program may use at most 64 MiB of HBM per device.

v0:
```python
import math
import jax
import jax.numpy as jnp
from jax import lax
from jax.sharding import PartitionSpec as P

D = 2048
HEADS = 16
EPS = 1e-05
THETA = 10000.0
NEGATIVE = -1e30


def rotate(vectors, placed_pos):
    head_size = vectors.shape[-1]
    half_dim = head_size // 2
    freqs = THETA ** (-jnp.arange(half_dim, dtype=jnp.float32) * 2.0 / head_size)
    angles = placed_pos.astype(jnp.float32)[..., None, None] * freqs
    cosine = jnp.cos(angles)
    sine = jnp.sin(angles)
    first_half = vectors[..., :half_dim]
    second_half = vectors[..., half_dim:]
    return jnp.concatenate(
        [first_half * cosine - second_half * sine, second_half * cosine + first_half * sine],
        axis=-1,
    )


def normalize(widened, row_sums, square_sums):
    row_mean = row_sums / D
    second_moment = square_sums / D
    inverse = 1.0 / jnp.sqrt(second_moment - row_mean * row_mean + EPS)
    return ((widened - row_mean[..., None]) * inverse[..., None]).astype(jnp.bfloat16)


def body(
    hidden_in,
    cache_keys,
    cache_values,
    lengths,
    query_weight,
    key_weight,
    value_weight,
    out_weight,
    gate_weight,
    up_weight,
    down_weight,
):
    requests, token_count, narrow_width = hidden_in.shape
    slot_count = cache_keys.shape[1]
    local_width = cache_keys.shape[2]
    head_size = D // HEADS
    local_heads = local_width // head_size
    score_scale = 1.0 / math.sqrt(head_size)
    shard_index = lax.axis_index("seq")
    slot_ids = shard_index * slot_count + jnp.arange(slot_count, dtype=jnp.int32)
    live_slots = slot_ids[None, :] < lengths[:, None]
    old_keys = cache_keys.reshape(requests, slot_count, local_heads, head_size)
    old_values = cache_values.reshape(requests, slot_count, local_heads, head_size).astype(
        jnp.float32
    )
    positions = lengths[:, None] + jnp.arange(token_count, dtype=jnp.int32)[None, :]
    out_list = []
    key_list = []
    value_list = []
    for token_step in range(token_count):
        row_block = hidden_in[:, token_step : token_step + 1]
        block_rows = row_block.shape[1]
        widened = row_block.astype(jnp.float32)
        row_sums, square_sums = lax.psum(
            (jnp.sum(widened, axis=-1), jnp.sum(widened * widened, axis=-1)), "seq"
        )
        normed = normalize(widened, row_sums, square_sums)
        query_part = jnp.einsum(
            "rnc,cm->rnm", normed, query_weight, preferred_element_type=jnp.float32
        )
        key_part = jnp.einsum("rnc,cm->rnm", normed, key_weight, preferred_element_type=jnp.float32)
        value_part = jnp.einsum(
            "rnc,cm->rnm", normed, value_weight, preferred_element_type=jnp.float32
        )
        queries, keys_full, values_full = lax.psum((query_part, key_part, value_part), "seq")
        placed_pos = positions[:, token_step : token_step + block_rows]
        queries = rotate(
            queries.reshape(requests, block_rows, local_heads, head_size), placed_pos
        ).astype(jnp.bfloat16)
        new_key = rotate(
            keys_full.reshape(requests, block_rows, local_heads, head_size), placed_pos
        ).astype(jnp.bfloat16)
        new_value = values_full.reshape(requests, block_rows, local_heads, head_size).astype(
            jnp.bfloat16
        )
        keys_new = jnp.concatenate(key_list + [new_key], axis=1)
        values_new = jnp.concatenate(value_list + [new_value], axis=1)
        old_scores = (
            jnp.einsum("rnhd,rjhd->rnhj", queries, old_keys, preferred_element_type=jnp.float32)
            * score_scale
        )
        old_scores = jnp.where(live_slots[:, None, None, :], old_scores, NEGATIVE)
        top_old = jnp.max(old_scores, axis=-1)
        weights_old = jnp.where(
            live_slots[:, None, None, :], jnp.exp(old_scores - top_old[..., None]), 0.0
        )
        total_old = jnp.sum(weights_old, axis=-1)
        summed_old = jnp.einsum(
            "rnhj,rjhd->rnhd", weights_old, old_values, precision=lax.Precision.HIGHEST
        )
        top_cache = lax.pmax(top_old, "seq")
        factor_old = jnp.exp(top_old - top_cache)
        total_cache, summed_cache = lax.psum(
            (total_old * factor_old, summed_old * factor_old[..., None]), "seq"
        )
        new_scores = (
            jnp.einsum("rnhd,rshd->rnhs", queries, keys_new, preferred_element_type=jnp.float32)
            * score_scale
        )
        key_index = jnp.arange(keys_new.shape[1], dtype=jnp.int32)
        query_index = token_step + jnp.arange(block_rows, dtype=jnp.int32)
        allowed = key_index[None, :] <= query_index[:, None]
        new_scores = jnp.where(allowed[None, :, None, :], new_scores, NEGATIVE)
        top_new = jnp.max(new_scores, axis=-1)
        weights_new = jnp.exp(new_scores - top_new[..., None])
        total_new = jnp.sum(weights_new, axis=-1)
        summed_new = jnp.einsum(
            "rnhs,rshd->rnhd",
            weights_new,
            values_new.astype(jnp.float32),
            precision=lax.Precision.HIGHEST,
        )
        top_score = jnp.maximum(top_cache, top_new)
        factor_cache = jnp.exp(top_cache - top_score)
        factor_new = jnp.exp(top_new - top_score)
        running = total_cache * factor_cache + total_new * factor_new
        combined = summed_cache * factor_cache[..., None] + summed_new * factor_new[..., None]
        attended = (
            (combined / running[..., None])
            .astype(jnp.bfloat16)
            .reshape(requests, block_rows, local_width)
        )
        attn_part = jnp.einsum(
            "rnm,mc->rnc", attended, out_weight, preferred_element_type=jnp.float32
        )
        mixed = widened + lax.psum(attn_part, "mdl")
        sums_mixed, squares_mixed = lax.psum(
            (jnp.sum(mixed, axis=-1), jnp.sum(mixed * mixed, axis=-1)), "seq"
        )
        normed2 = normalize(mixed, sums_mixed, squares_mixed)
        gate_part = jnp.einsum(
            "rnc,cf->rnf", normed2, gate_weight, preferred_element_type=jnp.float32
        )
        up_part = jnp.einsum("rnc,cf->rnf", normed2, up_weight, preferred_element_type=jnp.float32)
        gate_full, up_full = lax.psum((gate_part, up_part), "seq")
        act_full = (jax.nn.silu(gate_full) * up_full).astype(jnp.bfloat16)
        down_part = jnp.einsum(
            "rnf,fc->rnc", act_full, down_weight, preferred_element_type=jnp.float32
        )
        block_out = (mixed + lax.psum(down_part, "mdl")).astype(jnp.bfloat16)
        block_out, new_key, new_value = (block_out, new_key, new_value)
        out_list.append(block_out)
        key_list.append(new_key)
        value_list.append(new_value)
    hidden_out = jnp.concatenate(out_list, axis=1)
    keys_all = jnp.concatenate(key_list, axis=1)
    values_all = jnp.concatenate(value_list, axis=1)
    slot_hits = slot_ids[None, None, :] == positions[:, :, None]
    one_hot = slot_hits.astype(jnp.bfloat16)
    written = jnp.any(slot_hits, axis=1)[..., None]
    placed_keys = jnp.einsum(
        "rts,rtm->rsm",
        one_hot,
        keys_all.reshape(requests, token_count, local_width),
        preferred_element_type=jnp.float32,
    ).astype(jnp.bfloat16)
    placed_values = jnp.einsum(
        "rts,rtm->rsm",
        one_hot,
        values_all.reshape(requests, token_count, local_width),
        preferred_element_type=jnp.float32,
    ).astype(jnp.bfloat16)
    new_cache_keys = jnp.where(written, placed_keys, cache_keys)
    new_cache_values = jnp.where(written, placed_values, cache_values)
    return (hidden_out, new_cache_keys, new_cache_values)


def solution(mesh):
    placed = (
        P(None, None, "seq"),
        P(None, "seq", "mdl"),
        P(None, "seq", "mdl"),
        P(),
        P("seq", "mdl"),
        P("seq", "mdl"),
        P("seq", "mdl"),
        P("mdl", "seq"),
        P("seq", "mdl"),
        P("seq", "mdl"),
        P("mdl", "seq"),
    )
    return jax.shard_map(
        body,
        mesh=mesh,
        in_specs=placed,
        out_specs=(P(None, None, "seq"), P(None, "seq", "mdl"), P(None, "seq", "mdl")),
        check_vma=False,
    )
```

profile of v0, /device:TPU:0, one launch (start us, length us, event | category | flops | bytes accessed | tf_op | source)
XLA Modules:
  0.0 663.0 jit_solution(5343042440964158596)
XLA Ops:
  7.2 1.0 fusion.177
  8.5 43.5 %all-reduce.2 = (f32[32,1]{0,1:T(1,128)S(1)}, f32[32,1]{0,1:T(1,128)S(1)}, f32[32,1]{0,1:T(1,128)S(1)}, f32[32,1]{0,1:T(1,128)S(1)}, f32[32,1]{0,1:T(1,128)S(1)}...) all-reduce(f32[32,1]{0,1:T(1,128)S(1)} %bitcast.640, ...), channel_id=1, replica_groups=mesh['seq'=16,'mdl'=2] {'seq'}, use_global_device_ids=true, to_apply=%region_67.68 | all-reduce | flops 256 | bytes 2048 | tf_op jit(solution)/shard_map/psum | solution.py:70
  52.0 1.2 convolution_bitcast_fusion.10
  53.9 1.2 convolution_bitcast_fusion.19
  55.8 1.2 convolution_bitcast_fusion.16
  63.4 100.4 %all-reduce.20.cloned.1.call-done = (f32[32,1,8,128]{3,2,0,1:T(8,128)}, f32[32,1,8,128]{3,2,0,1:T(8,128)}, f32[32,1,8,128]{3,2,0,1:T(8,128)}, f32[32,1,8,128]{3,2,0,1:T(8,128)}) async-done(((f32[32,1,8,128]{3,2,0,1:T(8,128)}, f32[32,1,8,128]{3,2,0,1:T(8,128)}, f32[32,1,8,128]{3,2,0,1:T(8,128)}, f32[32,1,8,128]{3,2,0,1:T(8,128)}), (f32[32,1,8,128]{3,2,0,1:T(8,128)}, f32[32,1,8,128]{3,2,0,1:T(8,128)}, ...) | async-done | bytes 524304 | tf_op jit(solution)/shard_map/psum | solution.py:81
  163.8 1.2 fusion.71
  165.2 2.8 fusion.14
  168.2 1.2 fusion.12
  169.6 1.2 fusion.10
  171.0 1.2 fusion.8
  172.9 1.8 fusion
  174.6 1.8 fusion.2
  176.4 1.8 fusion.4
  178.2 1.8 fusion.6
  179.9 75.1 %all-reduce.6 = (f32[32,1,8]{2,0,1:T(8,128)S(1)}, f32[32,1,8]{2,0,1:T(8,128)S(1)}, f32[32,1,8]{2,0,1:T(8,128)S(1)}, f32[32,1,8]{2,0,1:T(8,128)S(1)}) all-reduce(f32[32,1,8]{2,0,1:T(8,128)S(1)} %bitcast.619, f32[32,1,8]{2,0,1:T(8,128)S(1)} %bitcast.618, f32[32,1,8]{2,0,1:T(8,128)S(1)} %bitcast.617, ...), channel_id=1, replica_groups=mesh['seq'=16,'mdl'=2] {'seq'}, use_global_device_ids=true, to_apply=%region_70.71 | all-reduce | flops 1024 | bytes 8192 | tf_op jit(solution)/shard_map/pmax | solution.py:107
  255.1 0.7 multiply_bitcast_fusion
  255.8 0.8 multiply_bitcast_fusion.1
  256.6 0.7 multiply_bitcast_fusion.2
  257.3 0.8 multiply_bitcast_fusion.3
  258.4 81.7 %all-reduce.25 = (bf16[32,1,1024]{2,0,1:T(8,128)(2,1)S(1)}, bf16[32,1,1024]{2,0,1:T(8,128)(2,1)S(1)}, bf16[32,1,1024]{2,0,1:T(8,128)(2,1)S(1)}, bf16[32,1,1024]{...) all-reduce(f32[32,1,1024]{2,0,1:T(8,128)S(1)} %convolution_bitcast_, ...), channel_id=1, replica_groups=mesh['seq'=16,'mdl'=2] {'seq'}, use_global_device_ids=true, to_apply=%region_74.75 | all-reduce | flops 132096 | bytes 794624 | tf_op jit(solution)/shard_map/psum | solution.py:81
  340.5 29.7 %all-reduce.18.cloned.1.call-done = (f32[32,1,8,128]{3,2,0,1:T(8,128)}, f32[32,1,8,128]{3,2,0,1:T(8,128)}, f32[32,1,8,128]{3,2,0,1:T(8,128)}, f32[32,1,8,128]{3,...) async-done(((f32[32,1,8,128]{3,2,0,1:T(8,128)}, f32[32,1,8,128]{3,2,0,1:T(8,128)}, ...) | async-done | bytes 1048592 | tf_op jit(solution)/shard_map/psum | solution.py:81
  370.1 1.1 multiply_subtract_fusion
  371.2 1.1 multiply_subtract_fusion.1
  372.3 1.1 multiply_subtract_fusion.2
  373.5 1.1 multiply_subtract_fusion.3
  379.1 0.8 copy.38
  379.8 1.1 fusion.36
  380.9 0.8 fusion.145
  381.9 0.8 convolution_bitcast_fusion.21
  382.7 1.0 fusion.40
  383.7 0.7 fusion.147
  384.6 0.8 convolution_bitcast_fusion.23
  385.6 1.0 fusion.55
  386.7 0.8 fusion.149
  387.7 0.8 convolution_bitcast_fusion.25
  388.7 0.7 fusion.151
  389.6 0.8 convolution_bitcast_fusion.27
  390.5 17.2 %all-reduce.24.cloned.1.call-done = (f32[32,1,128]{2,0,1:T(8,128)}, f32[32,1,128]{2,0,1:T(8,128)}, f32[32,1,128]{2,0,1:T(8,128)}, f32[32,1,128]{2,0,1:T(8,128)}) async-done(((f32[32,1,128]{2,0,1:T(8,128)}, f32[32,1,128]{2,0,1:T(8,128)}, f32[32,1,128]{2,0,1:T(8,128)}, f32[32,1,128]{2,0,1:T(8,128)}), (f32[32,1,128]{2,0,1:T(8,128)}, f32[32,1,128]{2,0,1:T(8,128)}, f32[32,1,128]{2,0,1:T(8,128)}, ...) | async-done | bytes 65552 | tf_op jit(solution)/shard_map/psum | solution.py:142
  407.7 0.8 fusion.155
  408.5 0.8 fusion.154
  409.3 0.8 fusion.153
  410.2 0.8 fusion.152
  411.0 42.0 %all-reduce = (f32[32,1]{0,1:T(1,128)S(1)}, f32[32,1]{0,1:T(1,128)S(1)}, f32[32,1]{0,1:T(1,128)S(1)}, f32[32,1]{0,1:T(1,128)S(1)}, f32[32,1]{0,1:T(1,128)S(1)}, ...) all-reduce(f32[32,1]{0,1:T(1,128)S(1)} %bitcast.648, ...), channel_id=1, replica_groups=mesh['seq'=16,'mdl'=2] {'seq'}, use_global_device_ids=true, to_apply=%region_82.83 | all-reduce | flops 256 | bytes 2048 | tf_op jit(solution)/shard_map/psum | solution.py:143
  453.0 0.8 fusion.131
  453.8 1.1 convolution_bitcast_fusion
  454.9 1.1 convolution_bitcast_fusion.1
  456.1 1.1 convolution_bitcast_fusion.2
  457.2 1.1 convolution_bitcast_fusion.3
  458.3 1.1 convolution_bitcast_fusion.4
  459.4 1.1 convolution_bitcast_fusion.5
  460.6 1.1 convolution_bitcast_fusion.6
  461.7 1.1 convolution_bitcast_fusion.7
  463.0 0.9 copy.42
  463.9 0.8 compare_reduce_fusion
  464.7 1.0 pad_maximum_fusion.2
  465.7 3.3 convert_select_fusion
  469.1 161.2 %all-reduce.16.cloned.1.call-done = (f32[32,1,4096]{2,0,1:T(8,128)}, f32[32,1,4096]{2,0,1:T(8,128)}, f32[32,1,4096]{2,0,1:T(8,128)}, f32[32,1,4096]{2,0,1:T(8,12...) async-done(((f32[32,1,4096]{2,0,1:T(8,128)}, f32[32,1,4096]{2,0,1:T(8,128)}, f32[32,1,4096]{2,0,1:T(8,128)}, ...) | async-done | bytes 4194320 | tf_op jit(solution)/shard_map/psum | solution.py:151
  630.3 2.6 convolution_bitcast_fusion.20
  632.9 0.9 convolution_bitcast_fusion.22
  634.1 0.9 convolution_bitcast_fusion.24
  635.1 0.9 convolution_bitcast_fusion.26
  636.1 3.7 convert_select_fusion.1
  639.7 13.2 %all-reduce.22.cloned.1.call-done = (f32[32,1,128]{2,0,1:T(8,128)}, f32[32,1,128]{2,0,1:T(8,128)}, f32[32,1,128]{2,0,1:T(8,128)}, f32[32,1,128]{2,0,1:T(8,128)}) async-done(((f32[32,1,128]{2,0,1:T(8,128)}, f32[32,1,128]{2,0,1:T(8,128)}, f32[32,1,128]{2,0,1:T(8,128)}, f32[32,1,128]{2,0,1:T(8,128)}), (f32[32,1,128]{2,0,1:T(8,128)}, f32[32,1,128]{2,0,1:T(8,128)}, f32[32,1,128]{2,0,1:T(8,128)}, ...) | async-done | bytes 65552 | tf_op jit(solution)/shard_map/psum | solution.py:156
  (206 shorter events, 20.2 us)
Async XLA Ops:
  7.2 446.6 %copy-start = (bf16[128,4096]{1,0:T(8,128)(2,1)S(1)}, bf16[128,4096]{1,0:T(8,128)(2,1)}, u32[]{:S(2)}) copy-start(bf16[128,4096]{1,0:T(8,128)(2,1)} %param.20) | copy-start | bytes 3145732
  7.2 50.5 %copy-start.2 = (bf16[128,1024]{1,0:T(8,128)(2,1)S(1)}, bf16[128,1024]{1,0:T(8,128)(2,1)}, u32[]{:S(2)}) copy-start(bf16[128,1024]{1,0:T(8,128)(2,1)} %param.15) | copy-start | bytes 786436
  7.2 51.5 %copy-start.3 = (bf16[128,1024]{1,0:T(8,128)(2,1)S(1)}, bf16[128,1024]{1,0:T(8,128)(2,1)}, u32[]{:S(2)}) copy-start(bf16[128,1024]{1,0:T(8,128)(2,1)} %param.16) | copy-start | bytes 786436
  7.2 156.6 %all-reduce.20.cloned.1.call-start = ((), (), s32[]{:S(2)}) async-start(), calls=%async_computation.2 | async-start | bytes 1048576 | tf_op jit(solution)/shard_map/psum | solution.py:81
  53.9 5.7 copy-start.4
  58.6 4.4 copy-start.37
  58.6 311.6 %all-reduce.18.cloned.1.call-start = ((), (), s32[]{:S(2)}) async-start(), calls=%async_computation.1 | async-start | bytes 2097152 | tf_op jit(solution)/shard_map/psum | solution.py:81
  62.9 102.1 %copy-start.32 = (s32[32,4]{0,1:T(4,128)}, s32[32,4]{0,1:T(4,128)S(1)}, u32[]{:S(2)}) copy-start(s32[32,4]{0,1:T(4,128)S(1)} %iota_add_fusion) | copy-start | bytes 1540
  63.0 102.1 %copy-start.35 = (s32[32]{0:T(128)}, s32[32]{0:T(128)S(1)}, u32[]{:S(2)}) copy-start(s32[32]{0:T(128)S(1)} %iota_add_fusion.1) | copy-start | bytes 388
  163.8 4.1 copy-start.10
  163.8 4.4 copy-start.38
  167.9 1.4 copy-start.9
  168.2 2.6 copy-start.23
  169.3 1.4 copy-start.8
  169.6 2.6 copy-start.25
  171.0 1.8 copy-start.27
  171.0 1.8 copy-start.6
  255.0 3.4 copy-start.30
  258.1 149.5 %all-reduce.24.cloned.1.call-start = ((), (), s32[]{:S(2)}) async-start(), calls=%async_computation.4 | async-start | bytes 131072 | tf_op jit(solution)/shard_map/psum | solution.py:142
  340.2 34.7 %copy-start.11 = (bf16[32,1,1024]{2,0,1:T(8,128)(2,1)}, bf16[32,1,1024]{2,0,1:T(8,128)(2,1)S(1)}, u32[]{:S(2)}) copy-start(bf16[32,1,1024]{2,0,1:T(8,128)(2,1)S(1)} %get-tuple-element.40) | copy-start | bytes 196612
  340.2 34.7 %copy-start.12 = (bf16[32,1,1024]{2,0,1:T(8,128)(2,1)}, bf16[32,1,1024]{2,0,1:T(8,128)(2,1)S(1)}, u32[]{:S(2)}) copy-start(bf16[32,1,1024]{2,0,1:T(8,128)(2,1)S(1)} %get-tuple-element.41) | copy-start | bytes 196612
  340.2 43.5 %copy-start.13 = (bf16[32,1,1024]{2,0,1:T(8,128)(2,1)}, bf16[32,1,1024]{2,0,1:T(8,128)(2,1)S(1)}, u32[]{:S(2)}) copy-start(bf16[32,1,1024]{2,0,1:T(8,128)(2,1)S(1)} %get-tuple-element.42) | copy-start | bytes 196612
  340.3 34.7 %copy-start.28 = (bf16[32,8,128,1]{2,1,0,3:T(8,128)(2,1)S(1)}, bf16[32,8,128,1]{2,1,0,3:T(8,128)(2,1)}, u32[]{:S(2)}) copy-start(bf16[32,8,128,1]{2,1,0,3:T(8,128)(2,1)} %copy-done.27) | copy-start | bytes 196612
  372.3 3.5 copy-start.26
  375.0 2.3 copy-start.24
  375.9 5.8 copy-start.22
  376.3 5.6 copy-start.5
  377.3 7.2 %copy-start.21 = (f32[32,1,8,128]{3,2,0,1:T(8,128)S(1)}, f32[32,1,8,128]{3,2,0,1:T(8,128)}, u32[]{:S(2)}) copy-start(f32[32,1,8,128]{3,2,0,1:T(8,128)} %get-tuple-element.69) | copy-start | bytes 393220
  380.9 5.8 copy-start.29
  380.9 6.6 copy-start.20
  382.7 6.0 copy-start.31
  382.7 6.7 %copy-start.19 = (f32[32,1,8,128]{3,2,0,1:T(8,128)S(1)}, f32[32,1,8,128]{3,2,0,1:T(8,128)}, u32[]{:S(2)}) copy-start(f32[32,1,8,128]{3,2,0,1:T(8,128)} %get-tuple-element.71) | copy-start | bytes 393220
  386.6 68.2 %copy-start.1 = (bf16[128,4096]{1,0:T(8,128)(2,1)S(1)}, bf16[128,4096]{1,0:T(8,128)(2,1)}, u32[]{:S(2)}) copy-start(bf16[128,4096]{1,0:T(8,128)(2,1)} %param.19) | copy-start | bytes 3145732
  390.4 239.9 %all-reduce.16.cloned.1.call-start = ((), (), s32[]{:S(2)}) async-start(), calls=%async_computation | async-start | bytes 8388608 | tf_op jit(solution)/shard_map/psum | solution.py:151
  407.7 48.3 %copy-start.16 = (f32[32,1,128]{2,0,1:T(8,128)S(1)}, f32[32,1,128]{2,0,1:T(8,128)}, u32[]{:S(2)}) copy-start(f32[32,1,128]{2,0,1:T(8,128)} %get-tuple-element.85) | copy-start | bytes 49156
  454.9 3.4 copy-start.15
  457.2 3.3 copy-start.14
  462.7 3.0 copy-start.7
  462.8 190.2 %all-reduce.22.cloned.1.call-start = ((), (), s32[]{:S(2)}) async-start(), calls=%async_computation.3 | async-start | bytes 131072 | tf_op jit(solution)/shard_map/psum | solution.py:156
  464.7 1.0 copy-start.33
  469.0 163.9 %copy-start.39 = (bf16[4096,128]{1,0:T(8,128)(2,1)S(1)}, bf16[4096,128]{1,0:T(8,128)(2,1)}, u32[]{:S(2)}) copy-start(bf16[4096,128]{1,0:T(8,128)(2,1)} %param.21) | copy-start | bytes 3145732
  630.3 2.6 copy-start.44
  630.3 2.6 copy-start.45
  632.9 1.0 copy-start.42
  632.9 1.2 copy-start.43
  633.8 1.2 copy-start.40
  633.8 1.3 copy-start.41
  635.0 1.0 copy-start.34
  635.0 1.0 copy-start.36
  636.0 16.9 %copy-start.18 = (f32[32,1,128]{2,0,1:T(8,128)S(1)}, f32[32,1,128]{2,0,1:T(8,128)}, u32[]{:S(2)}) copy-start(f32[32,1,128]{2,0,1:T(8,128)} %get-tuple-element.84) | copy-start | bytes 49156
  636.1 17.6 %copy-start.17 = (f32[32,1,128]{2,0,1:T(8,128)S(1)}, f32[32,1,128]{2,0,1:T(8,128)}, u32[]{:S(2)}) copy-start(f32[32,1,128]{2,0,1:T(8,128)} %get-tuple-element.85) | copy-start | bytes 49156
Sparse Core Ops, SparseCore 0:
  58.7 105.0 all-reduce.19
  258.2 111.8 all-reduce.17
  390.5 17.0 all-reduce.23
  462.9 167.3 all-reduce.15
  636.1 16.7 all-reduce.21
where the time goes:
time: 665 us; the launch traced here: 663 us
  waiting for transfers between devices  322 us (48%)
  blocking collectives  242 us (36%)
  matrix products  47.1 us (7%)
  other arithmetic  25.5 us (4%)
  between operations  14.6 us (2%)
  local copies, waits for them, and re-layouts  11.3 us (2%)
    psum x1, waiting for transfers between devices, body(): gate_full, up_full = lax.psum((gate_part, up_part), 'seq')  161 us
    psum x2, waiting for transfers between devices, body(): lax.psum((query_part, key_part, value_part), 'seq')  130 us
    psum x1, blocking collectives, body(): lax.psum((query_part, key_part, value_part), 'seq')  81.7 us
    pmax x1, blocking collectives, body(): top_cache = lax.pmax(top_old, 'seq')  75.1 us
    psum x1, blocking collectives, body(): lax.psum((jnp.sum(widened, axis=-1), jnp.sum(widened * widened, axis=-1))...  43.5 us
    psum x1, blocking collectives, body(): lax.psum((jnp.sum(mixed, axis=-1), jnp.sum(mixed * mixed, axis=-1)), 'seq')  42 us
    psum x1, waiting for transfers between devices, body(): mixed = widened + lax.psum(attn_part, 'mdl')  17.2 us
  transfers between devices with their start and end apart: 5, of which 5 were waited for; matrix products, arithmetic and copies ran while one was open for 2% of the time, Pallas kernels for 0%

commit v1 on v0

--- a/solution.py
+++ b/solution.py
@@ -9,6 +9,11 @@
 EPS = 1e-05
 THETA = 10000.0
 NEGATIVE = -1e30
+
+
+def gather_and_add(x, mesh_axis):
+    parts = lax.all_gather(x, mesh_axis)
+    return jnp.sum(parts, axis=0)
 
 
 def rotate(vectors, placed_pos):
@@ -139,7 +144,7 @@
         attn_part = jnp.einsum(
             "rnm,mc->rnc", attended, out_weight, preferred_element_type=jnp.float32
         )
-        mixed = widened + lax.psum(attn_part, "mdl")
+        mixed = widened + gather_and_add(attn_part, "mdl")
         sums_mixed, squares_mixed = lax.psum(
             (jnp.sum(mixed, axis=-1), jnp.sum(mixed * mixed, axis=-1)), "seq"
         )

time: 665 us -> 645 us (0.970)
  waiting for transfers between devices: 322 us -> 304 us
    psum x1 -> x0, waiting for transfers between devices: 17.2 us -> none  [body(): mixed = widened + lax.psum(attn_part, 'mdl')]
    all_gather x0 -> x4, blocking collectives: none -> 7.34 us  [gather_and_add(): parts = lax.all_gather(x, mesh_axis)]
  transfers between devices with their start and end apart: 5 -> 4, of which waited for: 5 -> 4; matrix products, arithmetic and copies ran while one was open for 2% -> 2% of each run, Pallas kernels for 0% -> 0%
where the time goes in v1:
time: 645 us; the launch traced here: 644 us
  waiting for transfers between devices  304 us (47%)
  blocking collectives  248 us (38%)
  matrix products  44.7 us (7%)
  other arithmetic  21 us (3%)
  between operations  14.7 us (2%)
  local copies, waits for them, and re-layouts  11.2 us (2%)
    psum x1, waiting for transfers between devices, body(): gate_full, up_full = lax.psum((gate_part, up_part), 'seq')  160 us
    psum x2, waiting for transfers between devices, body(): lax.psum((query_part, key_part, value_part), 'seq')  130 us
    psum x1, blocking collectives, body(): lax.psum((query_part, key_part, value_part), 'seq')  81.7 us
    pmax x1, blocking collectives, body(): top_cache = lax.pmax(top_old, 'seq')  75.1 us
    psum x1, blocking collectives, body(): lax.psum((jnp.sum(widened, axis=-1), jnp.sum(widened * widened, axis=-1))...  43.5 us
    psum x1, blocking collectives, body(): lax.psum((jnp.sum(mixed, axis=-1), jnp.sum(mixed * mixed, axis=-1)), 'seq')  40.1 us
    psum x1, waiting for transfers between devices, body(): block_out = (mixed + lax.psum(down_part, 'mdl')).astype(jnp.bfloat16)  13.2 us
  transfers between devices with their start and end apart: 4, of which 4 were waited for; matrix products, arithmetic and copies ran while one was open for 2% of the time, Pallas kernels for 0%

profile of v1, /device:TPU:0, one launch (start us, length us, event | category | flops | bytes accessed | tf_op | source)
XLA Modules:
  0.0 643.6 jit_solution(15725568454562260478)
XLA Ops:
  7.2 1.0 fusion.181
  8.5 43.5 %all-reduce.2 = (f32[32,1]{0,1:T(1,128)S(1)}, f32[32,1]{0,1:T(1,128)S(1)}, f32[32,1]{0,1:T(1,128)S(1)}, f32[32,1]{0,1:T(1,128)S(1)}, f32[32,1]{0,1:T(1,128)S(1)}...) all-reduce(f32[32,1]{0,1:T(1,128)S(1)} %bitcast.680, ...), channel_id=1, replica_groups=mesh['seq'=16,'mdl'=2] {'seq'}, use_global_device_ids=true, to_apply=%region_67.68 | all-reduce | flops 256 | bytes 2048 | tf_op jit(solution)/shard_map/psum | solution.py:75
  52.0 1.2 convolution_bitcast_fusion.10
  53.9 1.2 convolution_bitcast_fusion.19
  55.1 0.7 copy.92
  55.8 1.2 convolution_bitcast_fusion.16
  57.9 0.7 copy.101
  60.2 0.7 copy.106
  63.4 100.4 %all-reduce.18.cloned.1.call-done = (f32[32,1,8,128]{3,2,0,1:T(8,128)}, f32[32,1,8,128]{3,2,0,1:T(8,128)}, f32[32,1,8,128]{3,2,0,1:T(8,128)}, f32[32,1,8,128]{3,2,0,1:T(8,128)}) async-done(((f32[32,1,8,128]{3,2,0,1:T(8,128)}, f32[32,1,8,128]{3,2,0,1:T(8,128)}, f32[32,1,8,128]{3,2,0,1:T(8,128)}, f32[32,1,8,128]{3,2,0,1:T(8,128)}), (f32[32,1,8,128]{3,2,0,1:T(8,128)}, f32[32,1,8,128]{3,2,0,1:T(8,128)}, ...) | async-done | bytes 524304 | tf_op jit(solution)/shard_map/psum | solution.py:86
  163.8 1.2 fusion.71
  165.2 2.8 fusion.14
  168.2 1.2 fusion.12
  169.6 1.2 fusion.10
  171.0 1.2 fusion.8
  172.9 1.8 fusion
  174.6 1.8 fusion.2
  176.4 1.8 fusion.4
  178.2 1.8 fusion.6
  179.9 75.1 %all-reduce.6 = (f32[32,1,8]{2,0,1:T(8,128)S(1)}, f32[32,1,8]{2,0,1:T(8,128)S(1)}, f32[32,1,8]{2,0,1:T(8,128)S(1)}, f32[32,1,8]{2,0,1:T(8,128)S(1)}) all-reduce(f32[32,1,8]{2,0,1:T(8,128)S(1)} %bitcast.655, f32[32,1,8]{2,0,1:T(8,128)S(1)} %bitcast.654, f32[32,1,8]{2,0,1:T(8,128)S(1)} %bitcast.653, ...), channel_id=1, replica_groups=mesh['seq'=16,'mdl'=2] {'seq'}, use_global_device_ids=true, to_apply=%region_70.71 | all-reduce | flops 1024 | bytes 8192 | tf_op jit(solution)/shard_map/pmax | solution.py:112
  255.1 0.7 multiply_bitcast_fusion
  255.8 0.8 multiply_bitcast_fusion.1
  256.6 0.7 multiply_bitcast_fusion.2
  257.3 0.8 multiply_bitcast_fusion.3
  258.4 81.7 %all-reduce.21 = (bf16[32,1,1024]{2,0,1:T(8,128)(2,1)S(1)}, bf16[32,1,1024]{2,0,1:T(8,128)(2,1)S(1)}, bf16[32,1,1024]{2,0,1:T(8,128)(2,1)S(1)}, bf16[32,1,1024]{...) all-reduce(f32[32,1,1024]{2,0,1:T(8,128)S(1)} %convolution_bitcast_, ...), channel_id=1, replica_groups=mesh['seq'=16,'mdl'=2] {'seq'}, use_global_device_ids=true, to_apply=%region_74.75 | all-reduce | flops 132096 | bytes 794624 | tf_op jit(solution)/shard_map/psum | solution.py:86
  340.4 29.7 %all-reduce.16.cloned.1.call-done = (f32[32,1,8,128]{3,2,0,1:T(8,128)}, f32[32,1,8,128]{3,2,0,1:T(8,128)}, f32[32,1,8,128]{3,2,0,1:T(8,128)}, f32[32,1,8,128]{3,...) async-done(((f32[32,1,8,128]{3,2,0,1:T(8,128)}, f32[32,1,8,128]{3,2,0,1:T(8,128)}, ...) | async-done | bytes 1048592 | tf_op jit(solution)/shard_map/psum | solution.py:86
  370.1 1.1 multiply_subtract_fusion
  371.2 1.1 multiply_subtract_fusion.1
  372.3 1.1 multiply_subtract_fusion.2
  373.4 1.1 multiply_subtract_fusion.3
  377.4 0.7 copy.34
  378.3 1.1 fusion.36
  379.8 1.8 all-gather.3
  382.5 1.0 fusion.40
  383.9 1.8 all-gather.2
  385.7 0.7 fusion.158
  386.7 1.0 fusion.55
  387.7 0.8 fusion.153
  388.9 1.8 all-gather.1
  391.1 0.8 fusion.155
  392.2 1.8 all-gather
  394.2 40.1 %all-reduce = (f32[32,1]{0,1:T(1,128)S(1)}, f32[32,1]{0,1:T(1,128)S(1)}, f32[32,1]{0,1:T(1,128)S(1)}, f32[32,1]{0,1:T(1,128)S(1)}, f32[32,1]{0,1:T(1,128)S(1)}, ...) all-reduce(f32[32,1]{0,1:T(1,128)} %bitcast.688, ...), channel_id=1, replica_groups=mesh['seq'=16,'mdl'=2] {'seq'}, use_global_device_ids=true, to_apply=%region_82.83 | all-reduce | flops 256 | bytes 2048 | tf_op jit(solution)/shard_map/psum | solution.py:148
  434.4 1.1 convolution_bitcast_fusion
  435.5 1.1 convolution_bitcast_fusion.1
  436.6 1.1 convolution_bitcast_fusion.2
  437.7 1.1 convolution_bitcast_fusion.3
  438.9 1.1 convolution_bitcast_fusion.4
  440.0 1.1 convolution_bitcast_fusion.5
  441.1 1.1 convolution_bitcast_fusion.6
  442.2 1.1 convolution_bitcast_fusion.7
  443.6 1.5 copy.42
  445.1 0.9 compare_reduce_fusion
  446.0 0.9 pad_maximum_fusion.2
  446.9 3.4 convert_select_fusion
  450.4 160.4 %all-reduce.14.cloned.1.call-done = (f32[32,1,4096]{2,0,1:T(8,128)}, f32[32,1,4096]{2,0,1:T(8,128)}, f32[32,1,4096]{2,0,1:T(8,128)}, f32[32,1,4096]{2,0,1:T(8,12...) async-done(((f32[32,1,4096]{2,0,1:T(8,128)}, f32[32,1,4096]{2,0,1:T(8,128)}, f32[32,1,4096]{2,0,1:T(8,128)}, ...) | async-done | bytes 4194320 | tf_op jit(solution)/shard_map/psum | solution.py:156
  610.9 2.6 convolution_bitcast_fusion.20
  613.4 0.9 convolution_bitcast_fusion.21
  614.6 0.9 convolution_bitcast_fusion.22
  615.6 0.9 convolution_bitcast_fusion.23
  616.6 3.7 convert_select_fusion.1
  620.3 13.2 %all-reduce.20.cloned.1.call-done = (f32[32,1,128]{2,0,1:T(8,128)}, f32[32,1,128]{2,0,1:T(8,128)}, f32[32,1,128]{2,0,1:T(8,128)}, f32[32,1,128]{2,0,1:T(8,128)}) async-done(((f32[32,1,128]{2,0,1:T(8,128)}, f32[32,1,128]{2,0,1:T(8,128)}, f32[32,1,128]{2,0,1:T(8,128)}, f32[32,1,128]{2,0,1:T(8,128)}), (f32[32,1,128]{2,0,1:T(8,128)}, f32[32,1,128]{2,0,1:T(8,128)}, f32[32,1,128]{2,0,1:T(8,128)}, ...) | async-done | bytes 65552 | tf_op jit(solution)/shard_map/psum | solution.py:161
  633.5 0.7 add_convert_fusion.4
  634.2 0.7 add_convert_fusion.5
  635.0 0.7 add_convert_fusion.6
  635.7 0.7 add_convert_fusion.7
  (213 shorter events, 15.5 us)
Async XLA Ops:
  7.2 427.2 %copy-start = (bf16[128,4096]{1,0:T(8,128)(2,1)S(1)}, bf16[128,4096]{1,0:T(8,128)(2,1)}, u32[]{:S(2)}) copy-start(bf16[128,4096]{1,0:T(8,128)(2,1)} %param.20) | copy-start | bytes 3145732
  7.2 50.5 %copy-start.2 = (bf16[128,1024]{1,0:T(8,128)(2,1)S(1)}, bf16[128,1024]{1,0:T(8,128)(2,1)}, u32[]{:S(2)}) copy-start(bf16[128,1024]{1,0:T(8,128)(2,1)} %param.15) | copy-start | bytes 786436
  7.2 51.5 %copy-start.3 = (bf16[128,1024]{1,0:T(8,128)(2,1)S(1)}, bf16[128,1024]{1,0:T(8,128)(2,1)}, u32[]{:S(2)}) copy-start(bf16[128,1024]{1,0:T(8,128)(2,1)} %param.16) | copy-start | bytes 786436
  7.2 156.6 %all-reduce.18.cloned.1.call-start = ((), (), s32[]{:S(2)}) async-start(), calls=%async_computation.2 | async-start | bytes 1048576 | tf_op jit(solution)/shard_map/psum | solution.py:86
  53.9 5.7 copy-start.4
  58.6 4.4 copy-start.36
  58.6 311.5 %all-reduce.16.cloned.1.call-start = ((), (), s32[]{:S(2)}) async-start(), calls=%async_computation.1 | async-start | bytes 2097152 | tf_op jit(solution)/shard_map/psum | solution.py:86
  62.9 102.1 %copy-start.29 = (s32[32,4]{0,1:T(4,128)}, s32[32,4]{0,1:T(4,128)S(1)}, u32[]{:S(2)}) copy-start(s32[32,4]{0,1:T(4,128)S(1)} %iota_add_fusion) | copy-start | bytes 1540
  63.0 102.1 %copy-start.34 = (s32[32]{0:T(128)}, s32[32]{0:T(128)S(1)}, u32[]{:S(2)}) copy-start(s32[32]{0:T(128)S(1)} %iota_add_fusion.1) | copy-start | bytes 388
  163.8 4.1 copy-start.10
  163.8 4.4 copy-start.39
  167.9 1.4 copy-start.9
  168.2 2.6 copy-start.21
  169.3 1.4 copy-start.8
  169.6 2.6 copy-start.23
  171.0 1.8 copy-start.25
  171.0 1.8 copy-start.6
  255.0 3.4 copy-start.28
  258.1 352.7 %all-reduce.14.cloned.1.call-start = ((), (), s32[]{:S(2)}) async-start(), calls=%async_computation | async-start | bytes 8388608 | tf_op jit(solution)/shard_map/psum | solution.py:156
  340.1 34.7 %copy-start.13 = (bf16[32,1,1024]{2,0,1:T(8,128)(2,1)}, bf16[32,1,1024]{2,0,1:T(8,128)(2,1)S(1)}, u32[]{:S(2)}) copy-start(bf16[32,1,1024]{2,0,1:T(8,128)(2,1)S(1)} %get-tuple-element.40) | copy-start | bytes 196612
  340.2 34.7 %copy-start.14 = (bf16[32,1,1024]{2,0,1:T(8,128)(2,1)}, bf16[32,1,1024]{2,0,1:T(8,128)(2,1)S(1)}, u32[]{:S(2)}) copy-start(bf16[32,1,1024]{2,0,1:T(8,128)(2,1)S(1)} %get-tuple-element.41) | copy-start | bytes 196612
  340.2 43.4 %copy-start.15 = (bf16[32,1,1024]{2,0,1:T(8,128)(2,1)}, bf16[32,1,1024]{2,0,1:T(8,128)(2,1)S(1)}, u32[]{:S(2)}) copy-start(bf16[32,1,1024]{2,0,1:T(8,128)(2,1)S(1)} %get-tuple-element.42) | copy-start | bytes 196612
  340.3 34.7 %copy-start.26 = (bf16[32,8,128,1]{2,1,0,3:T(8,128)(2,1)S(1)}, bf16[32,8,128,1]{2,1,0,3:T(8,128)(2,1)}, u32[]{:S(2)}) copy-start(bf16[32,8,128,1]{2,1,0,3:T(8,128)(2,1)} %copy-done.25) | copy-start | bytes 196612
  372.3 3.5 copy-start.24
  374.9 1.8 copy-start.22
  375.8 3.6 copy-start.20
  376.3 3.1 copy-start.31
  376.3 3.4 copy-start.5
  376.7 6.8 %copy-start.30 = (f32[32,1,8]{2,0,1:T(8,128)S(1)}, f32[32,1,8]{2,0,1:T(8,128)}, u32[]{:S(2)}) copy-start(f32[32,1,8]{2,0,1:T(8,128)} %get-tuple-element.45) | copy-start | bytes 3076
  377.1 6.4 %copy-start.19 = (f32[32,1,8,128]{3,2,0,1:T(8,128)S(1)}, f32[32,1,8,128]{3,2,0,1:T(8,128)}, u32[]{:S(2)}) copy-start(f32[32,1,8,128]{3,2,0,1:T(8,128)} %get-tuple-element.69) | copy-start | bytes 393220
  379.4 8.3 %copy-start.27 = (f32[32,8]{1,0:T(8,128)S(1)}, f32[32,8]{1,0:T(8,128)}, u32[]{:S(2)}) copy-start(f32[32,8]{1,0:T(8,128)} %copy.34) | copy-start | bytes 3076
  379.4 9.1 %copy-start.18 = (f32[32,1,8,128]{3,2,0,1:T(8,128)S(1)}, f32[32,1,8,128]{3,2,0,1:T(8,128)}, u32[]{:S(2)}) copy-start(f32[32,1,8,128]{3,2,0,1:T(8,128)} %get-tuple-element.70) | copy-start | bytes 393220
  382.5 9.3 %copy-start.17 = (f32[32,1,8,128]{3,2,0,1:T(8,128)S(1)}, f32[32,1,8,128]{3,2,0,1:T(8,128)}, u32[]{:S(2)}) copy-start(f32[32,1,8,128]{3,2,0,1:T(8,128)} %get-tuple-element.71) | copy-start | bytes 393220
  387.7 47.8 %copy-start.1 = (bf16[128,4096]{1,0:T(8,128)(2,1)S(1)}, bf16[128,4096]{1,0:T(8,128)(2,1)}, u32[]{:S(2)}) copy-start(bf16[128,4096]{1,0:T(8,128)(2,1)} %param.19) | copy-start | bytes 3145732
  388.5 5.6 copy-start.37
  388.5 5.6 copy-start.38
  394.0 47.0 %copy-start.11 = (f32[32,128]{1,0:T(8,128)}, f32[32,128]{1,0:T(8,128)S(1)}, u32[]{:S(2)}) copy-start(f32[32,128]{1,0:T(8,128)S(1)} %reduce.48) | copy-start | bytes 49156
  443.3 3.6 copy-start.7
  443.3 190.2 %all-reduce.20.cloned.1.call-start = ((), (), s32[]{:S(2)}) async-start(), calls=%async_computation.3 | async-start | bytes 131072 | tf_op jit(solution)/shard_map/psum | solution.py:161
  446.0 1.0 copy-start.32
  450.3 163.1 %copy-start.40 = (bf16[4096,128]{1,0:T(8,128)(2,1)S(1)}, bf16[4096,128]{1,0:T(8,128)(2,1)}, u32[]{:S(2)}) copy-start(bf16[4096,128]{1,0:T(8,128)(2,1)} %param.21) | copy-start | bytes 3145732
  610.9 2.6 copy-start.45
  610.9 2.6 copy-start.46
  613.4 1.0 copy-start.43
  613.4 1.2 copy-start.44
  614.4 1.2 copy-start.41
  614.4 1.3 copy-start.42
  615.6 1.0 copy-start.16
  615.6 1.0 copy-start.33
  615.6 1.0 copy-start.35
  616.6 19.1 %copy-start.12 = (f32[32,128]{1,0:T(8,128)S(1)}, f32[32,128]{1,0:T(8,128)}, u32[]{:S(2)}) copy-start(f32[32,128]{1,0:T(8,128)} %copy-done.11) | copy-start | bytes 49156
Sparse Core Ops, SparseCore 0:
  58.7 105.0 all-reduce.17
  258.2 111.8 all-reduce.15
  443.5 167.3 all-reduce.13
  616.7 16.7 all-reduce.19
